TPU v7x, 32 devices: a whole 2x2x4 slice. The times are simulated.
32 devices in a mesh: runner: 4 (over z), cells: 8 (over y, x, core).
Axes of the slice: x: 2, y: 2, z: 4, core: 2. Of those that a mesh axis runs over, the one named last changes fastest.
Arguments:
- states: float32 [512, 64, 128], P('runner', 'cells'), may hold values from -4 to 4
- diffusivity: float32 [64, 128], P('cells'), may hold values from 0.03 to 0.2
- velocity: float32 [2, 64, 128], P(None, 'cells'), may hold values from -0.15 to 0.15
- counts: int32 [4], replicated, may hold values from 1 to 128, 256 in all
- obs_index: int32 [4096], P('cells'), may hold values from 0 to 1023
- obs_value: float32 [4096], P('cells'), may hold values from -6 to 6
- obs_weight: float32 [4096], P('cells'), may hold values from 0.3 to 3
Outputs:
- analysed: float32 [512, 64, 128], P('runner', 'cells')
Inputs may be any that keep to these rules, and one draw needn't show every extreme that they name: Runner r's members fill its first counts[r] slots, in runner order; the counts sum to 256 and the largest is exactly 128. Observation k lies in the rows of cells index k // 512; obs_index counts cells within those 8 x 128 cells, row by row; a cell may be observed more than once.
All inputs are finite; a program needn't handle non-finite values.
Results may differ from a plain program's by a relative error of at most 0.013.
Values may be sent and summed in bfloat16 or wider, within the bound.
No kernel may reach another device: no remote copies, remote signals or barrier semaphores. Data moves between devices by JAX's collectives and lax.ppermute only.
A program may use at most 64 MiB of HBM per device.

v0:
```python
import jax
import jax.numpy as jnp
from jax import lax
from jax.sharding import PartitionSpec as P

STEPS = 4


def with_halo(block, sides, width):
    for axis, dim in sides:
        count = lax.axis_size(axis)
        forward = [(i, i + 1) for i in range(count - 1)]
        forward.append((count - 1, 0))
        backward = [(target, source) for source, target in forward]
        low = lax.ppermute(
            lax.slice_in_dim(block, block.shape[dim] - width, None, axis=dim), axis, forward
        )
        high = lax.ppermute(lax.slice_in_dim(block, 0, width, axis=dim), axis, backward)
        block = jnp.concatenate([low, block, high], axis=dim)
    return block


def update(values, upper_row, lower_row, diffusivity, velocity_rows, velocity_cols):
    right_col = jnp.roll(values, -1, axis=2)
    left_col = jnp.roll(values, 1, axis=2)
    laplace = upper_row + lower_row + right_col + left_col - 4.0 * values
    return (
        values
        + diffusivity * laplace
        - 0.5 * velocity_rows * (upper_row - lower_row)
        - 0.5 * velocity_cols * (right_col - left_col)
        - 0.05 * values * values * values
    )


def body(states, diffusivity, velocity, counts, obs_index, obs_value, obs_weight):
    runners = lax.axis_size("runner")
    slot_count = states.shape[0]
    rows_own = states.shape[1]
    members = slot_count // 2 * runners
    values = states
    extended = with_halo(values, (("cells", 1),), STEPS)
    fields = jnp.concatenate([diffusivity[None], velocity], axis=0)
    wide_fields = with_halo(fields, (("cells", 1),), STEPS)
    for iteration in range(STEPS):
        inner = extended.shape[1] - 2
        first = iteration + 1
        local = wide_fields[:, first : first + inner, :]
        extended = update(
            extended[:, 1:-1, :],
            extended[:, 2:, :],
            extended[:, :-2, :],
            local[0],
            local[1],
            local[2],
        )
    values = extended
    runner_rank = lax.axis_index("runner")
    run_ends = jnp.cumsum(counts)
    offsets = run_ends - counts
    run_ids = jnp.arange(runners, dtype=jnp.int32)
    picker = run_ids == runner_rank
    own_count = jnp.sum(jnp.where(picker, counts, 0))
    own_base = jnp.sum(jnp.where(picker, offsets, 0))
    position = jnp.arange(slot_count, dtype=jnp.int32)
    is_live = position < own_count
    flat_rows = values.reshape(slot_count, -1)
    live_sum = jnp.sum(jnp.where(is_live[:, None], flat_rows, 0.0), axis=0)
    ensemble_mean = lax.psum(live_sum, "runner") / members
    member_deviation = jnp.where(is_live[:, None], flat_rows - ensemble_mean, 0.0).astype(
        jnp.bfloat16
    )
    member_ids = jnp.arange(members, dtype=jnp.int32)
    owner_run = jnp.sum((run_ends[None, :] <= member_ids[:, None]).astype(jnp.int32), axis=1)
    owner_off = jnp.sum(
        jnp.where(owner_run[:, None] == run_ids[None, :], offsets[None, :], 0), axis=1
    )
    slot_of = owner_run * slot_count + member_ids - owner_off
    own_obs = jnp.take(member_deviation, obs_index, axis=1)
    gathered = lax.all_gather(member_deviation, "runner", axis=0, tiled=True)
    compact = jnp.take(gathered, slot_of, axis=0)
    observed = jnp.take(compact, obs_index, axis=1)
    weighted = (own_obs.astype(jnp.float32) * obs_weight).astype(jnp.bfloat16)
    gram_part = lax.dot_general(
        weighted, observed, (((1,), (1,)), ((), ())), preferred_element_type=jnp.float32
    )
    innovation = obs_value - jnp.take(ensemble_mean, obs_index)
    bias_part = jnp.dot(weighted.astype(jnp.float32), innovation, precision=lax.Precision.HIGHEST)
    gram_rows, bias_rows = lax.psum((gram_part, bias_part), "cells")
    member_col = own_base + position
    trace_sum = lax.psum(
        jnp.sum(weighted.astype(jnp.float32) * own_obs.astype(jnp.float32)), ("runner", "cells")
    )
    scaling = members / trace_sum
    scaled_own = (gram_rows * scaling).astype(jnp.bfloat16)
    bias_own = (bias_rows * scaling).astype(jnp.bfloat16)
    scaled_all, bias_all = (
        lax.all_gather(scaled_own, "runner", axis=0, tiled=True),
        lax.all_gather(bias_own, "runner", axis=0, tiled=True),
    )
    scaled_full = jnp.take(scaled_all, slot_of, axis=0)
    bias_full = jnp.take(bias_all, slot_of, axis=0)
    square = jnp.dot(scaled_own, scaled_full, preferred_element_type=jnp.float32).astype(
        jnp.bfloat16
    )
    cubed = jnp.dot(square, scaled_full, preferred_element_type=jnp.float32)
    identity = jnp.where(
        is_live[:, None] & (member_ids[None, :] == member_col[:, None]), 1.0, 0.0
    ).astype(jnp.float32)
    transform = (
        1.0 * identity
        - 0.5 * scaled_own.astype(jnp.float32)
        + 0.375 * square.astype(jnp.float32)
        - 0.3125 * cubed
    )
    shift_weights = jnp.dot(
        transform, bias_full.astype(jnp.float32), precision=lax.Precision.HIGHEST
    )
    increment = lax.psum(
        jnp.dot(
            shift_weights, member_deviation.astype(jnp.float32), precision=lax.Precision.HIGHEST
        ),
        "runner",
    )
    narrow = transform.astype(jnp.bfloat16)
    applied = jnp.dot(narrow, compact, preferred_element_type=jnp.float32)
    result = jnp.where(is_live[:, None], ensemble_mean + increment + applied, 0.0)
    return result.reshape(slot_count, rows_own, -1)


def solution(mesh):
    return jax.shard_map(
        body,
        mesh=mesh,
        in_specs=(
            P("runner", "cells", None),
            P("cells", None),
            P(None, "cells", None),
            P(),
            P("cells"),
            P("cells"),
            P("cells"),
        ),
        out_specs=P("runner", "cells", None),
        check_vma=False,
    )
```

profile of v0, /device:TPU:0, one launch (start us, length us, event | category | flops | bytes accessed | tf_op | source)
XLA Modules:
  0.0 205.1 jit_solution(15974762030387377627)
XLA Ops:
  6.5 0.8 fusion.23
  7.8 2.9 %collective-permute-start.3 = (f32[3,4,128]{2,1,0:T(4,128)S(1)}, f32[3,4,128]{2,1,0:T(4,128)S(1)}, u32[]{:S(2)}, u32[]{:S(2)}) collective-permute-start(f32[3,4,128]{2,1,0:T(4,128)S(1)} %get-tuple-element.41), channel_id=1, source_target_pairs={{1,0},{2,1},{3,2},{4,3},{5,4},{6,5},{7,6},{0,7},{9,8},{10,9},{11,1... | collective-permute-start | bytes 18440 | tf_op jit(solution)/shard_map/ppermute | solution.py:18
  10.7 1.3 fusion.41
  12.1 2.6 %collective-permute-start.1 = (f32[128,4,128]{2,1,0:T(4,128)S(1)}, f32[128,4,128]{2,1,0:T(4,128)S(1)}, u32[]{:S(2)}, u32[]{:S(2)}) collective-permute-start(f32[128,4,128]{2,1,0:T(4,128)S(1)} %get-tuple-element.30), channel_id=1, source_target_pairs={{1,0},{2,1},{3,2},{4,3},{5,4},{6,5},{7,6},{0,7},{9,8},{10,9},{11,1... | collective-permute-start | bytes 786440 | tf_op jit(solution)/shard_map/ppermute | solution.py:18
  14.8 0.7 copy-done.4
  15.4 0.7 copy-done.7
  16.3 0.7 fusion.25
  17.2 0.6 iota_compare_fusion.3
  17.9 2.1 %collective-permute-done = f32[128,4,128]{2,1,0:T(4,128)S(1)} collective-permute-done((f32[128,4,128]{2,1,0:T(4,128)S(1)}, f32[128,4,128]{2,1,0:T(4,128)S(1)}, u32[]{:S(2)}, u32[]{:S(2)}) %collective-permute-start) | collective-permute-done | bytes 262176 | tf_op jit(solution)/shard_map/ppermute | solution.py:15
  20.9 1.2 fusion.3
  22.8 1.2 fusion.4
  24.7 1.2 fusion.5
  27.0 13.4 %psum.35 = f32[1024]{0:T(1024)S(1)} all-reduce(f32[1024]{0:T(1024)S(1)} %bitcast.75), channel_id=1, replica_groups=mesh['runner'=4,'cells'=8] {'runner'}, use_global_device_ids=true, to_apply=%region_2.3 | all-reduce | flops 1024 | bytes 8192 | tf_op jit(solution)/shard_map/psum | solution.py:69
  40.4 0.8 fusion.8
  41.3 0.8 copy-done
  42.3 2.3 %gather_fusion.4 = f32[512]{0:T(512)S(1)} fusion(f32[1024]{0:T(1024)S(1)} %broadcast_multiply_fusion, s32[1024]{0:T(1024)S(1)} %pad_clamp_fusion.1), kind=kCustom, calls=%fused_computation.4 | custom fusion | bytes 6144 | tf_op jit(solution)/shard_map/jit(_take)/gather | solution.py:87
  44.6 1.3 gather_fusion
  46.0 0.8 fusion.10
  46.8 38.3 %psum.37 = f32[]{:T(128)} all-reduce(f32[]{:T(128)} %fusion.10), channel_id=1, replica_groups=mesh['runner'=4,'cells'=8] {'runner','cells'}, use_global_device_ids=true, to_apply=%region_9.10 | all-reduce | flops 1 | bytes 8 | tf_op jit(solution)/shard_map/psum | solution.py:91
  86.1 12.9 %psum.38 = f32[128]{0:T(128)S(1)} all-reduce(f32[128]{0:T(128)S(1)} %convolution_bitcast_fusion), channel_id=1, replica_groups=mesh['runner'=4,'cells'=8] {'cells'}, use_global_device_ids=true, to_apply=%region_10.11 | all-reduce | flops 128 | bytes 1024 | tf_op jit(solution)/shard_map/psum | solution.py:89
  99.0 9.9 %all-gather = bf16[4,1,128]{2,1,0:T(2,128)(2,1)S(1)} all-gather(bf16[1,1,128]{2,1,0:T(2,128)(2,1)S(1)} %convert_bitcast_fusion), channel_id=1, replica_groups=mesh['runner'=4,'cells'=8] {'runner'}, dimensions={0}, use_global_device_ids=true | all-gather | bytes 1280 | tf_op jit(solution)/shard_map/all_gather | solution.py:99
  108.9 1.9 gather_fusion.5
  110.9 2.9 %gather_fusion.1 = bf16[256,1024]{1,0:T(8,128)(2,1)S(1)} fusion(bf16[512,1024]{1,0:T(8,128)(2,1)} %all-gather.3.cloned.1.call-done, s32[1024]{0:T(1024)S(1)} %pad_clamp_fusion), kind=kCustom, calls=%fused_computation.1 | custom fusion | bytes 1049600 | tf_op jit(solution)/shard_map/jit(_take)/gather | solution.py:81
  114.2 2.0 gather_fusion.2
  116.1 1.1 fusion.11
  117.2 0.7 iota_add_fusion
  118.0 50.6 %all-reduce.2.cloned.1.call-done = f32[128,256]{1,0:T(8,128)} async-done(((f32[128,256]{1,0:T(8,128)}), f32[128,256]{1,0:T(8,128)}) %all-reduce.2.cloned.1.call-update) | async-done | bytes 131088 | tf_op jit(solution)/shard_map/psum | solution.py:89
  168.5 0.9 multiply_convert_fusion
  169.4 13.9 %all_gather.10 = bf16[512,256]{1,0:T(8,128)(2,1)S(1)} all-gather(bf16[128,256]{1,0:T(8,128)(2,1)S(1)} %multiply_convert_fusion), channel_id=1, replica_groups=mesh['runner'=4,'cells'=8] {'runner'}, dimensions={0}, use_global_device_ids=true | all-gather | bytes 327680 | tf_op jit(solution)/shard_map/all_gather | solution.py:98
  183.4 1.2 gather_fusion.3
  185.4 11.7 %psum.39 = f32[1024]{0:T(1024)S(1)} all-reduce(f32[1024]{0:T(1024)S(1)} %bitcast.74), channel_id=1, replica_groups=mesh['runner'=4,'cells'=8] {'runner'}, use_global_device_ids=true, to_apply=%region_11.12 | all-reduce | flops 1024 | bytes 8192 | tf_op jit(solution)/shard_map/psum | solution.py:119
  197.4 0.9 copy.17
  (62 shorter events, 6.5 us)
Async XLA Ops:
  6.5 104.4 %all-gather.3.cloned.1.call-start = ((), (), s32[]{:S(2)}) async-start(), calls=%async_computation | async-start | bytes 1310720 | tf_op jit(solution)/shard_map/all_gather | solution.py:80
  7.3 10.5 %collective-permute-start.2 = (f32[3,4,128]{2,1,0:T(4,128)S(1)}, f32[3,4,128]{2,1,0:T(4,128)S(1)}, u32[]{:S(2)}, u32[]{:S(2)}) collective-permute-start(f32[3,4,128]{2,1,0:T(4,128)S(1)} %get-tuple-element.40), channel_id=1, source_target_pairs={{0,1},{1,2},{2,3},{3,4},{4,5},{5,6},{6,7},{7,0},{8,9},{9,10},{10,1... | collective-permute-start | bytes 18440 | tf_op jit(solution)/shard_map/ppermute | solution.py:15
  7.8 12.2 %copy-start.1 = (f32[128,8,128]{2,1,0:T(8,128)S(1)}, f32[128,8,128]{2,1,0:T(8,128)}, u32[]{:S(2)}) copy-start(f32[128,8,128]{2,1,0:T(8,128)} %param.7) | copy-start | bytes 1572868
  7.8 10.0 %collective-permute-start.3 = (f32[3,4,128]{2,1,0:T(4,128)S(1)}, f32[3,4,128]{2,1,0:T(4,128)S(1)}, u32[]{:S(2)}, u32[]{:S(2)}) collective-permute-start(f32[3,4,128]{2,1,0:T(4,128)S(1)} %get-tuple-element.41), channel_id=1, source_target_pairs={{1,0},{2,1},{3,2},{4,3},{5,4},{6,5},{7,6},{0,7},{9,8},{10,9},{11,1... | collective-permute-start | bytes 18440 | tf_op jit(solution)/shard_map/ppermute | solution.py:18
  10.7 4.0 %copy-start.2 = (f32[2,8,128]{2,1,0:T(8,128)S(1)}, f32[2,8,128]{2,1,0:T(8,128)}, u32[]{:S(2)}) copy-start(f32[2,8,128]{2,1,0:T(8,128)} %param.9) | copy-start | bytes 24580
  12.0 7.9 %collective-permute-start = (f32[128,4,128]{2,1,0:T(4,128)S(1)}, f32[128,4,128]{2,1,0:T(4,128)S(1)}, u32[]{:S(2)}, u32[]{:S(2)}) collective-permute-start(f32[128,4,128]{2,1,0:T(4,128)S(1)} %get-tuple-element.29), channel_id=1, source_target_pairs={{0,1},{1,2},{2,3},{3,4},{4,5},{5,6},{6,7},{7,0},{8,9},{9,10},{10,1... | collective-permute-start | bytes 786440 | tf_op jit(solution)/shard_map/ppermute | solution.py:15
  12.1 7.8 %collective-permute-start.1 = (f32[128,4,128]{2,1,0:T(4,128)S(1)}, f32[128,4,128]{2,1,0:T(4,128)S(1)}, u32[]{:S(2)}, u32[]{:S(2)}) collective-permute-start(f32[128,4,128]{2,1,0:T(4,128)S(1)} %get-tuple-element.30), channel_id=1, source_target_pairs={{1,0},{2,1},{3,2},{4,3},{5,4},{6,5},{7,6},{0,7},{9,8},{10,9},{11,1... | collective-permute-start | bytes 786440 | tf_op jit(solution)/shard_map/ppermute | solution.py:18
  14.8 0.7 copy-start.4
  15.4 0.7 copy-start.7
  17.1 0.8 copy-start.3
  41.2 0.9 copy-start
  41.2 127.3 %all-reduce.2.cloned.1.call-start = ((), (), s32[]{:S(2)}) async-start(), calls=%async_computation.1 | async-start | bytes 262144 | tf_op jit(solution)/shard_map/psum | solution.py:89
  44.6 1.4 copy-start.6
  44.6 1.4 copy-start.5
Sparse Core Ops, SparseCore 0:
  41.3 26.5 all-gather.2
  117.4 51.1 all-reduce.1
where the time goes:
time: 206 us; the launch traced here: 205 us
  blocking collectives  100 us (49%)
  waiting for transfers between devices  52.7 us (26%)
  local copies, waits for them, and re-layouts  18.9 us (9%)
  between operations  14.3 us (7%)
  other arithmetic  10.4 us (5%)
  starting transfers between devices  6.15 us (3%)
  matrix products  2.57 us (1%)
    psum x1, waiting for transfers between devices, body(): gram_rows, bias_rows = lax.psum((gram_part, bias_part), 'cells')  50.6 us
    psum x1, blocking collectives, body(): lax.psum(jnp.sum(weighted.astype(jnp.float32) * own_obs.astype(jnp.float3...  38.3 us
    all_gather x1, blocking collectives, body(): lax.all_gather(scaled_own, 'runner', axis=0, tiled=True)  13.9 us
    psum x1, blocking collectives, body(): ensemble_mean = lax.psum(live_sum, 'runner') / members  13.4 us
    psum x1, blocking collectives, body(): gram_rows, bias_rows = lax.psum((gram_part, bias_part), 'cells')  12.9 us
    psum x1, blocking collectives, body(): lax.psum(jnp.dot(shift_weights, member_deviation.astype(jnp.float32), pre...  11.7 us
    all_gather x1, blocking collectives, body(): lax.all_gather(bias_own, 'runner', axis=0, tiled=True)  9.94 us
    ppermute x2, starting transfers between devices, with_halo(): lax.ppermute(lax.slice_in_dim(block, 0, width, axis=dim), axis, backward)  5.56 us
  transfers between devices with their start and end apart: 6, of which 2 were waited for; matrix products, arithmetic and copies ran while one was open for 5% of the time, Pallas kernels for 0%

commit v1 on v0

--- a/solution.py
+++ b/solution.py
@@ -4,6 +4,23 @@
 from jax.sharding import PartitionSpec as P
 
 STEPS = 4
+
+
+def in_order(blocks, dim):
+    shape = list(blocks.shape[1:])
+    shape[dim] *= blocks.shape[0]
+    return jnp.moveaxis(blocks, 0, dim).reshape(shape)
+
+
+def collect(value, axis, dim):
+    devices = lax.axis_size(axis)
+    ahead = [(i, (i + 1) % devices) for i in range(devices)]
+    blocks = [value]
+    while len(blocks) < devices:
+        blocks.append(lax.ppermute(blocks[-1], axis, ahead))
+    index = lax.axis_index(axis)
+    blocks = jnp.stack(blocks)[(index - jnp.arange(devices)) % devices]
+    return in_order(blocks, dim)
 
 
 def with_halo(block, sides, width):
@@ -95,7 +112,7 @@
     scaled_own = (gram_rows * scaling).astype(jnp.bfloat16)
     bias_own = (bias_rows * scaling).astype(jnp.bfloat16)
     scaled_all, bias_all = (
-        lax.all_gather(scaled_own, "runner", axis=0, tiled=True),
+        collect(scaled_own, "runner", 0),
         lax.all_gather(bias_own, "runner", axis=0, tiled=True),
     )
     scaled_full = jnp.take(scaled_all, slot_of, axis=0)

time: 206 us -> 208 us (level)
  blocking collectives: 100 us -> 82.9 us
  waiting for transfers between devices: 52.7 us -> 69.4 us
    ppermute x0 -> x3, waiting for transfers between devices: none -> 16 us  [collect(): blocks.append(lax.ppermute(blocks[-1], axis, ahead))]
    all_gather x1 -> x0, blocking collectives: 13.9 us -> none  [body(): lax.all_gather(scaled_own, 'runner', axis=0, tiled=True)]
    psum x1, blocking collectives: 11.7 us -> 8.35 us  [body(): lax.psum(jnp.dot(shift_weights, member_deviation.astype(jnp.float32), pre...]
  transfers between devices with their start and end apart: 6 -> 9, of which waited for: 2 -> 5; matrix products, arithmetic and copies ran while one was open for 5% -> 5% of each run, Pallas kernels for 0% -> 0%
where the time goes in v1:
time: 208 us; the launch traced here: 207 us
  blocking collectives  82.9 us (40%)
  waiting for transfers between devices  69.4 us (33%)
  local copies, waits for them, and re-layouts  19.5 us (9%)
  between operations  14.4 us (7%)
  other arithmetic  10.4 us (5%)
  starting transfers between devices  7.69 us (4%)
  matrix products  2.57 us (1%)
    psum x1, waiting for transfers between devices, body(): gram_rows, bias_rows = lax.psum((gram_part, bias_part), 'cells')  51.2 us
    psum x1, blocking collectives, body(): lax.psum(jnp.sum(weighted.astype(jnp.float32) * own_obs.astype(jnp.float3...  38.4 us
    ppermute x3, waiting for transfers between devices, collect(): blocks.append(lax.ppermute(blocks[-1], axis, ahead))  16 us
    psum x1, blocking collectives, body(): ensemble_mean = lax.psum(live_sum, 'runner') / members  13.4 us
    psum x1, blocking collectives, body(): gram_rows, bias_rows = lax.psum((gram_part, bias_part), 'cells')  12.9 us
    all_gather x1, blocking collectives, body(): lax.all_gather(bias_own, 'runner', axis=0, tiled=True)  9.9 us
    psum x1, blocking collectives, body(): lax.psum(jnp.dot(shift_weights, member_deviation.astype(jnp.float32), pre...  8.35 us
    ppermute x2, starting transfers between devices, with_halo(): lax.ppermute(lax.slice_in_dim(block, 0, width, axis=dim), axis, backward)  5.56 us
  transfers between devices with their start and end apart: 9, of which 5 were waited for; matrix products, arithmetic and copies ran while one was open for 5% of the time, Pallas kernels for 0%

profile of v1, /device:TPU:0, one launch (start us, length us, event | category | flops | bytes accessed | tf_op | source)
XLA Modules:
  0.0 207.0 jit_solution(7652261775394831259)
XLA Ops:
  6.5 0.8 fusion.23
  7.8 2.9 %collective-permute-start.3 = (f32[3,4,128]{2,1,0:T(4,128)S(1)}, f32[3,4,128]{2,1,0:T(4,128)S(1)}, u32[]{:S(2)}, u32[]{:S(2)}) collective-permute-start(f32[3,4,128]{2,1,0:T(4,128)S(1)} %get-tuple-element.41), channel_id=1, source_target_pairs={{1,0},{2,1},{3,2},{4,3},{5,4},{6,5},{7,6},{0,7},{9,8},{10,9},{11,1... | collective-permute-start | bytes 18440 | tf_op jit(solution)/shard_map/ppermute | solution.py:35
  10.7 1.3 fusion.43
  12.1 2.6 %collective-permute-start.1 = (f32[128,4,128]{2,1,0:T(4,128)S(1)}, f32[128,4,128]{2,1,0:T(4,128)S(1)}, u32[]{:S(2)}, u32[]{:S(2)}) collective-permute-start(f32[128,4,128]{2,1,0:T(4,128)S(1)} %get-tuple-element.30), channel_id=1, source_target_pairs={{1,0},{2,1},{3,2},{4,3},{5,4},{6,5},{7,6},{0,7},{9,8},{10,9},{11,1... | collective-permute-start | bytes 786440 | tf_op jit(solution)/shard_map/ppermute | solution.py:35
  14.8 0.7 copy-done.5
  16.3 0.7 fusion.25
  17.9 2.1 %collective-permute-done = f32[128,4,128]{2,1,0:T(4,128)S(1)} collective-permute-done((f32[128,4,128]{2,1,0:T(4,128)S(1)}, f32[128,4,128]{2,1,0:T(4,128)S(1)}, u32[]{:S(2)}, u32[]{:S(2)}) %collective-permute-start) | collective-permute-done | bytes 262176 | tf_op jit(solution)/shard_map/ppermute | solution.py:32
  20.9 1.2 fusion.3
  22.8 1.2 fusion.4
  24.7 1.2 fusion.5
  27.0 13.4 %psum.35 = f32[1024]{0:T(1024)S(1)} all-reduce(f32[1024]{0:T(1024)S(1)} %bitcast.87), channel_id=1, replica_groups=mesh['runner'=4,'cells'=8] {'runner'}, use_global_device_ids=true, to_apply=%region_2.3 | all-reduce | flops 1024 | bytes 8192 | tf_op jit(solution)/shard_map/psum | solution.py:86
  40.4 0.8 fusion.8
  41.3 0.8 copy-done
  42.3 2.3 %gather_fusion.5 = f32[512]{0:T(512)S(1)} fusion(f32[1024]{0:T(1024)S(1)} %broadcast_multiply_fusion, s32[1024]{0:T(1024)S(1)} %pad_clamp_fusion.2), kind=kCustom, calls=%fused_computation.5 | custom fusion | bytes 6144 | tf_op jit(solution)/shard_map/jit(_take)/gather | solution.py:104
  44.6 1.3 gather_fusion
  46.0 0.9 fusion.10
  46.9 38.4 %psum.37 = f32[]{:T(128)} all-reduce(f32[]{:T(128)} %fusion.10), channel_id=1, replica_groups=mesh['runner'=4,'cells'=8] {'runner','cells'}, use_global_device_ids=true, to_apply=%region_9.10 | all-reduce | flops 1 | bytes 8 | tf_op jit(solution)/shard_map/psum | solution.py:108
  86.3 12.9 %psum.38 = f32[128]{0:T(128)S(1)} all-reduce(f32[128]{0:T(128)S(1)} %convolution_bitcast_fusion), channel_id=1, replica_groups=mesh['runner'=4,'cells'=8] {'cells'}, use_global_device_ids=true, to_apply=%region_10.11 | all-reduce | flops 128 | bytes 1024 | tf_op jit(solution)/shard_map/psum | solution.py:106
  99.3 9.9 %all-gather = bf16[4,1,128]{2,1,0:T(2,128)(2,1)S(1)} all-gather(bf16[1,1,128]{2,1,0:T(2,128)(2,1)S(1)} %convert_bitcast_fusion), channel_id=1, replica_groups=mesh['runner'=4,'cells'=8] {'runner'}, dimensions={0}, use_global_device_ids=true | all-gather | bytes 1280 | tf_op jit(solution)/shard_map/all_gather | solution.py:116
  109.2 1.9 gather_fusion.6
  111.2 2.9 %gather_fusion.1 = bf16[256,1024]{1,0:T(8,128)(2,1)S(1)} fusion(bf16[512,1024]{1,0:T(8,128)(2,1)} %all-gather.3.cloned.1.call-done, s32[1024]{0:T(1024)S(1)} %pad_clamp_fusion.1), kind=kCustom, calls=%fused_computation.1 | custom fusion | bytes 1049600 | tf_op jit(solution)/shard_map/jit(_take)/gather | solution.py:98
  114.4 2.0 gather_fusion.2
  116.4 1.1 fusion.11
  117.5 51.2 %all-reduce.2.cloned.1.call-done = f32[128,256]{1,0:T(8,128)} async-done(((f32[128,256]{1,0:T(8,128)}), f32[128,256]{1,0:T(8,128)}) %all-reduce.2.cloned.1.call-update) | async-done | bytes 131088 | tf_op jit(solution)/shard_map/psum | solution.py:106
  168.8 1.0 multiply_convert_fusion
  169.8 1.5 collective-permute-start.4
  171.3 4.6 %collective-permute-done.4 = bf16[128,256]{1,0:T(8,128)(2,1)S(1)} collective-permute-done((bf16[128,256]{1,0:T(8,128)(2,1)S(1)}, bf16[128,256]{1,0:T(8,128)(2,1)S(1)}, u32[]{:S(2)}, u32[]{:S(2)}) %collective-permute-start.4) | collective-permute-done | bytes 65568 | tf_op jit(solution)/shard_map/ppermute | solution.py:20
  176.5 5.4 %collective-permute-done.5 = bf16[128,256]{1,0:T(8,128)(2,1)S(1)} collective-permute-done((bf16[128,256]{1,0:T(8,128)(2,1)S(1)}, bf16[128,256]{1,0:T(8,128)(2,1)S(1)}, u32[]{:S(2)}, u32[]{:S(2)}) %collective-permute-start.5) | collective-permute-done | bytes 65568 | tf_op jit(solution)/shard_map/ppermute | solution.py:20
  182.0 6.0 %collective-permute-done.6 = bf16[128,256]{1,0:T(8,128)(2,1)S(1)} collective-permute-done((bf16[128,256]{1,0:T(8,128)(2,1)S(1)}, bf16[128,256]{1,0:T(8,128)(2,1)S(1)}, u32[]{:S(2)}, u32[]{:S(2)}) %collective-permute-start.6) | collective-permute-done | bytes 65568 | tf_op jit(solution)/shard_map/ppermute | solution.py:20
  188.6 1.2 gather_fusion.4
  190.7 8.3 %psum.39 = f32[1024]{0:T(1024)S(1)} all-reduce(f32[1024]{0:T(1024)S(1)} %bitcast.86), channel_id=1, replica_groups=mesh['runner'=4,'cells'=8] {'runner'}, use_global_device_ids=true, to_apply=%region_11.12 | all-reduce | flops 1024 | bytes 8192 | tf_op jit(solution)/shard_map/psum | solution.py:136
  199.3 0.9 copy.17
  (74 shorter events, 9.0 us)
Async XLA Ops:
  6.5 104.6 %all-gather.3.cloned.1.call-start = ((), (), s32[]{:S(2)}) async-start(), calls=%async_computation | async-start | bytes 1310720 | tf_op jit(solution)/shard_map/all_gather | solution.py:97
  7.3 10.4 %collective-permute-start.2 = (f32[3,4,128]{2,1,0:T(4,128)S(1)}, f32[3,4,128]{2,1,0:T(4,128)S(1)}, u32[]{:S(2)}, u32[]{:S(2)}) collective-permute-start(f32[3,4,128]{2,1,0:T(4,128)S(1)} %get-tuple-element.40), channel_id=1, source_target_pairs={{0,1},{1,2},{2,3},{3,4},{4,5},{5,6},{6,7},{7,0},{8,9},{9,10},{10,1... | collective-permute-start | bytes 18440 | tf_op jit(solution)/shard_map/ppermute | solution.py:32
  7.8 12.2 %copy-start.1 = (f32[128,8,128]{2,1,0:T(8,128)S(1)}, f32[128,8,128]{2,1,0:T(8,128)}, u32[]{:S(2)}) copy-start(f32[128,8,128]{2,1,0:T(8,128)} %param.7) | copy-start | bytes 1572868
  7.8 10.0 %collective-permute-start.3 = (f32[3,4,128]{2,1,0:T(4,128)S(1)}, f32[3,4,128]{2,1,0:T(4,128)S(1)}, u32[]{:S(2)}, u32[]{:S(2)}) collective-permute-start(f32[3,4,128]{2,1,0:T(4,128)S(1)} %get-tuple-element.41), channel_id=1, source_target_pairs={{1,0},{2,1},{3,2},{4,3},{5,4},{6,5},{7,6},{0,7},{9,8},{10,9},{11,1... | collective-permute-start | bytes 18440 | tf_op jit(solution)/shard_map/ppermute | solution.py:35
  10.7 4.0 %copy-start.3 = (f32[2,8,128]{2,1,0:T(8,128)S(1)}, f32[2,8,128]{2,1,0:T(8,128)}, u32[]{:S(2)}) copy-start(f32[2,8,128]{2,1,0:T(8,128)} %param.9) | copy-start | bytes 24580
  12.0 7.9 %collective-permute-start = (f32[128,4,128]{2,1,0:T(4,128)S(1)}, f32[128,4,128]{2,1,0:T(4,128)S(1)}, u32[]{:S(2)}, u32[]{:S(2)}) collective-permute-start(f32[128,4,128]{2,1,0:T(4,128)S(1)} %get-tuple-element.29), channel_id=1, source_target_pairs={{0,1},{1,2},{2,3},{3,4},{4,5},{5,6},{6,7},{7,0},{8,9},{9,10},{10,1... | collective-permute-start | bytes 786440 | tf_op jit(solution)/shard_map/ppermute | solution.py:32
  12.1 7.8 %collective-permute-start.1 = (f32[128,4,128]{2,1,0:T(4,128)S(1)}, f32[128,4,128]{2,1,0:T(4,128)S(1)}, u32[]{:S(2)}, u32[]{:S(2)}) collective-permute-start(f32[128,4,128]{2,1,0:T(4,128)S(1)} %get-tuple-element.30), channel_id=1, source_target_pairs={{1,0},{2,1},{3,2},{4,3},{5,4},{6,5},{7,6},{0,7},{9,8},{10,9},{11,1... | collective-permute-start | bytes 786440 | tf_op jit(solution)/shard_map/ppermute | solution.py:35
  14.8 0.7 copy-start.5
  15.4 0.7 copy-start.8
  17.0 0.8 copy-start.4
  41.2 0.9 copy-start
  41.2 127.6 %all-reduce.2.cloned.1.call-start = ((), (), s32[]{:S(2)}) async-start(), calls=%async_computation.1 | async-start | bytes 262144 | tf_op jit(solution)/shard_map/psum | solution.py:106
  44.6 1.4 copy-start.7
  44.6 1.4 copy-start.6
  168.8 13.2 %copy-start.2 = (f32[128,256]{1,0:T(8,128)S(1)}, f32[128,256]{1,0:T(8,128)}, u32[]{:S(2)}) copy-start(f32[128,256]{1,0:T(8,128)} %all-reduce.2.cloned.1.call-done) | copy-start | bytes 393220
  169.8 6.1 %collective-permute-start.4 = (bf16[128,256]{1,0:T(8,128)(2,1)S(1)}, bf16[128,256]{1,0:T(8,128)(2,1)S(1)}, u32[]{:S(2)}, u32[]{:S(2)}) collective-permute-start(bf16[128,256]{1,0:T(8,128)(2,1)S(1)} %multiply_convert_fusion), channel_id=1, source_target_pairs={{0,8},{8,16},{16,24},{24,0},{1,9},{9,17},{17,25},{25,1},{2,10},{10... | collective-permute-start | bytes 196616 | tf_op jit(solution)/shard_map/ppermute | solution.py:20
  175.9 6.1 %collective-permute-start.5 = (bf16[128,256]{1,0:T(8,128)(2,1)S(1)}, bf16[128,256]{1,0:T(8,128)(2,1)S(1)}, u32[]{:S(2)}, u32[]{:S(2)}) collective-permute-start(bf16[128,256]{1,0:T(8,128)(2,1)S(1)} %collective-permute-done.4), channel_id=1, source_target_pairs={{0,8},{8,16},{16,24},{24,0},{1,9},{9,17},{17,25},{25,1},{2,10},{10... | collective-permute-start | bytes 196616 | tf_op jit(solution)/shard_map/ppermute | solution.py:20
  182.0 6.1 %collective-permute-start.6 = (bf16[128,256]{1,0:T(8,128)(2,1)S(1)}, bf16[128,256]{1,0:T(8,128)(2,1)S(1)}, u32[]{:S(2)}, u32[]{:S(2)}) collective-permute-start(bf16[128,256]{1,0:T(8,128)(2,1)S(1)} %collective-permute-done.5), channel_id=1, source_target_pairs={{0,8},{8,16},{16,24},{24,0},{1,9},{9,17},{17,25},{25,1},{2,10},{10... | collective-permute-start | bytes 196616 | tf_op jit(solution)/shard_map/ppermute | solution.py:20
Sparse Core Ops, SparseCore 0:
  41.3 26.5 all-gather.2
  117.6 51.0 all-reduce.1
